TPU v7x, 128 devices: a whole 4x4x4 slice. The times are simulated.
128 devices in a mesh: cuts: 8 (over y, core), fsdp: 16 (over z, x).
Axes of the slice: x: 4, y: 4, z: 4, core: 2. Of those that a mesh axis runs over, the one named last changes fastest.
Arguments:
- hidden_states: bfloat16 [65536, 8192], P(('cuts', 'fsdp')), may hold values from -1200 to 1200
- key_cotangent: bfloat16 [65536, 512], P(('cuts', 'fsdp')), may hold values from -60 to 60
- old_weight: bfloat16 [16384, 256], P(('cuts', 'fsdp')), may hold values from -0.0625 to 0.0625
- old_first: bfloat16 [16384, 256], P(('cuts', 'fsdp')), may hold values from -1 to 1
- old_first_scale: float32 [16384], P(('cuts', 'fsdp')), may hold values from 3e-05 to 0.0003
- old_second: bfloat16 [16384, 256], P(('cuts', 'fsdp')), may hold values from 0 to 1
- old_second_scale: float32 [16384], P(('cuts', 'fsdp')), may hold values from 1e-08 to 1e-07
- send_counts: int32 [128, 128], P(('cuts', 'fsdp')), may hold values from 0 to 2, as said below
Outputs:
- input_grad: bfloat16 [65536, 8192], P(('cuts', 'fsdp'))
- new_weight: bfloat16 [8192, 512], P(('cuts', 'fsdp'))
- first_code: bfloat16 [8192, 512], P(('cuts', 'fsdp'))
- first_scale: float32 [8192, 2], P(('cuts', 'fsdp'))
- second_code: bfloat16 [8192, 512], P(('cuts', 'fsdp'))
- second_scale: float32 [8192, 2], P(('cuts', 'fsdp'))
Inputs may be any that keep to these rules, and one draw needn't show every extreme that they name: Every row and every column of send_counts sums to 128; each entry is 0, 1 or 2, and every row and every column holds 2 exactly once.
All inputs are finite; a program needn't handle non-finite values.
Results may differ from a plain program's by a relative error of at most 0.00075.
Values may be sent and summed in bfloat16 or wider, within the bound.
A program may use at most 128 MiB of HBM per device.

v0:
```python
import jax
import jax.numpy as jnp
from jax import lax
from jax.sharding import PartitionSpec as P

STEP = 2000
beta_first = 0.9
beta_second = 0.95
adam_epsilon = 1e-05
learn_rate = 0.001
weight_decay = 0.1
clip_norm = 1.0
tiny_scale = 1e-30


def adam_blocks(clipped, weight, first, first_scale, second, second_scale):
    m_old = first.astype(jnp.float32) * first_scale[:, None]
    v_old = second.astype(jnp.float32) * second_scale[:, None]
    m_new = beta_first * m_old + (1.0 - beta_first) * clipped
    v_new = beta_second * v_old + (1.0 - beta_second) * clipped * clipped
    m_hat = m_new / (1.0 - beta_first**STEP)
    v_hat = v_new / (1.0 - beta_second**STEP)
    w_old = weight.astype(jnp.float32)
    w_new = (
        w_old - learn_rate * (m_hat / (jnp.sqrt(v_hat) + adam_epsilon) + weight_decay * w_old)
    ).astype(jnp.bfloat16)
    m_scale = jnp.max(jnp.abs(m_new), axis=1) + tiny_scale
    v_scale = jnp.max(v_new, axis=1) + tiny_scale
    m_code = (m_new / m_scale[:, None]).astype(jnp.bfloat16)
    v_code = (v_new / v_scale[:, None]).astype(jnp.bfloat16)
    return (w_new, m_code, m_scale, v_code, v_scale)


def shards(
    hidden_states,
    key_cotangent,
    old_weight,
    old_first,
    old_first_scale,
    old_second,
    old_second_scale,
    send_counts,
):
    peer_count = lax.axis_size(("cuts", "fsdp"))
    slot_count = old_weight.shape[0]
    block_size = old_weight.shape[1]
    key_width = key_cotangent.shape[1]
    peer_slots = 2 * slot_count // peer_count
    own_rows = slot_count * block_size // key_width
    row_counts = send_counts[0]
    slot_ends = jnp.cumsum(row_counts)
    starts = slot_ends - row_counts
    lane_index = jnp.arange(peer_slots, dtype=jnp.int32)
    live_slots = lane_index[None, :] < row_counts[:, None]
    pick_index = jnp.where(live_slots, starts[:, None] + lane_index[None, :], 0)
    stacked = jnp.stack([old_weight, old_first, old_second], axis=1)
    scales = jnp.stack([old_first_scale, old_second_scale], axis=1)
    packed = stacked[pick_index]
    packed_scales = scales[pick_index]
    tallies = row_counts.astype(jnp.float32)[:, None]
    arrived = lax.all_to_all(packed, ("cuts", "fsdp"), split_axis=0, concat_axis=0, tiled=True)
    arrived_scales, arrived_tallies = (
        lax.all_to_all(packed_scales, ("cuts", "fsdp"), split_axis=0, concat_axis=0, tiled=True),
        lax.all_to_all(tallies, ("cuts", "fsdp"), split_axis=0, concat_axis=0, tiled=True),
    )
    got_counts = arrived_tallies[:, 0].astype(jnp.int32)
    offsets = jnp.cumsum(got_counts) - got_counts
    live_here = lane_index[None, :] < got_counts[:, None]
    target = jnp.where(live_here, offsets[:, None] + lane_index[None, :], slot_count).reshape(-1)
    owned_state = (
        jnp.zeros((slot_count, 3, block_size), jnp.bfloat16)
        .at[target]
        .set(arrived.reshape(-1, 3, block_size), mode="drop")
    )
    owned_scales = (
        jnp.zeros((slot_count, 2), jnp.float32)
        .at[target]
        .set(arrived_scales.reshape(-1, 2), mode="drop")
    )
    own_weight = owned_state[:, 0].reshape(own_rows, key_width)
    input_grad = lax.dot_general(
        key_cotangent,
        lax.all_gather(own_weight, ("cuts", "fsdp"), axis=0, tiled=True),
        (((1,), (1,)), ((), ())),
        preferred_element_type=jnp.float32,
    ).astype(jnp.bfloat16)
    gradient = lax.psum_scatter(
        lax.dot_general(
            hidden_states,
            key_cotangent,
            (((0,), (0,)), ((), ())),
            preferred_element_type=jnp.float32,
        ),
        ("cuts", "fsdp"),
        scatter_dimension=0,
        tiled=True,
    )
    token_total = hidden_states.shape[0] * peer_count
    gradient = gradient / token_total
    square_sum = lax.psum(jnp.sum(gradient * gradient), ("cuts", "fsdp"))
    factor = jnp.minimum(1.0, clip_norm / (jnp.sqrt(square_sum) + 1e-06))
    clipped = (gradient * factor).reshape(slot_count, block_size)
    w_new, m_code, m_scale, v_code, v_scale = adam_blocks(
        clipped,
        owned_state[:, 0],
        owned_state[:, 1],
        owned_scales[:, 0],
        owned_state[:, 2],
        owned_scales[:, 1],
    )
    blocks_row = key_width // block_size
    return (
        input_grad,
        w_new.reshape(own_rows, key_width),
        m_code.reshape(own_rows, key_width),
        m_scale.reshape(own_rows, blocks_row),
        v_code.reshape(own_rows, key_width),
        v_scale.reshape(own_rows, blocks_row),
    )


def solution(mesh):
    placed = (
        P(("cuts", "fsdp"), None),
        P(("cuts", "fsdp"), None),
        P(("cuts", "fsdp"), None),
        P(("cuts", "fsdp"), None),
        P(("cuts", "fsdp")),
        P(("cuts", "fsdp"), None),
        P(("cuts", "fsdp")),
        P(("cuts", "fsdp"), None),
    )
    return jax.shard_map(
        shards,
        mesh=mesh,
        in_specs=placed,
        out_specs=(
            P(("cuts", "fsdp"), None),
            P(("cuts", "fsdp"), None),
            P(("cuts", "fsdp"), None),
            P(("cuts", "fsdp"), None),
            P(("cuts", "fsdp"), None),
            P(("cuts", "fsdp"), None),
        ),
        check_vma=False,
    )
```

profile of v0, /device:TPU:1, one launch (start us, length us, event | category | flops | bytes accessed | tf_op | source)
XLA Modules:
  0.0 894.5 jit_solution(2391013964506324690)
XLA Ops:
  8.6 11.5 %all-to-all-start = ((f32[128,1,1]{2,1,0:T(1,128)}), f32[128,1,1]{2,1,0:T(1,128)S(1)}, u32[]{:S(2)}, u32[]{:S(2)}) async-start(f32[128,1,1]{2,1,0:T(1,128)} %copy.60), calls=%async_computation | async-start | bytes 131072 | tf_op jit(solution)/shard_map/all_to_all | solution.py:64
  20.1 0.8 copy.65
  22.7 0.9 copy.62
  23.7 0.9 copy.63
  24.6 0.9 copy.64
  26.1 1.2 gather_fusion
  27.2 1.1 copy.66
  28.3 1.5 all-to-all-done
  29.9 8.2 all-to-all-start.1
  38.5 2.4 convert_reduce_fusion
  41.1 9.7 %all-to-all-done.1 = bf16[128,2,3,256]{3,1,2,0:T(2,128)(2,1)S(1)} async-done(((bf16[128,2,3,256]{3,1,2,0:T(2,128)(2,1)}), bf16[128,2,3,256]{3,1,2,0:T(2,128)(2,1)S(1)}, u32[]{:S(2)}, u32[]{:S(2)}) %all-to-all-start.1) | async-done | bytes 393248 | tf_op jit(solution)/shard_map/all_to_all | solution.py:61
  51.1 7.3 scatter_fusion
  59.7 11.7 %fusion.15 = f32[8192,512]{1,0:T(8,128)} fusion(bf16[512,8192]{1,0:T(8,128)(2,1)} %param.8, bf16[512,512]{1,0:T(8,128)(2,1)S(1)} %copy-done), kind=kOutput, calls=%fused_computation.49 | convolution fusion | flops 4294967296 | bytes 25690112 | tf_op jit(solution)/shard_map/dot_general | solution.py:88
  73.0 0.9 copy.71
  73.8 14.2 %all_to_all.16 = f32[128,2,2]{1,2,0:T(2,128)S(1)} all-to-all(f32[128,2,2]{1,2,0:T(2,128)S(1)} %copy.71), channel_id=1, replica_groups=mesh['cuts'=8,'fsdp'=16] {'cuts','fsdp'}, dimensions={0} | all-to-all | bytes 4096 | tf_op jit(solution)/shard_map/all_to_all | solution.py:63
  88.1 0.9 copy.78
  88.9 1.3 scatter_custom_fusion.1
  91.6 34.0 %all-gather.2.cloned.1.call-done = bf16[8192,512]{1,0:T(8,128)(2,1)} async-done(((bf16[64,512]{1,0:T(8,128)(2,1)}), bf16[8192,512]{1,0:T(8,128)(2,1)}) %all-gather.2.cloned.1.call-update) | async-done | bytes 8388624 | tf_op jit(solution)/shard_map/all_gather | solution.py:83
  125.6 10.2 %fusion = bf16[512,8192]{0,1:T(8,128)(2,1)} fusion(bf16[8192,512]{1,0:T(8,128)(2,1)} %all-gather.2.cloned.1.call-done, bf16[512,512]{1,0:T(8,128)(2,1)S(1)} %copy-done), kind=kOutput, calls=%fused_computation.5 | convolution fusion | flops 4299161600 | bytes 17301504 | tf_op jit(solution)/shard_map/dot_general | solution.py:81
  135.8 640.2 %reduce-scatter.2.cloned.1.call-done = f32[64,512]{1,0:T(8,128)} async-done(((f32[8192,512]{1,0:T(8,128)}), f32[64,512]{1,0:T(8,128)}) %reduce-scatter.2.cloned.1.call-update) | async-done | bytes 131088 | tf_op jit(solution)/shard_map/reduce_scatter | solution.py:87
  776.0 1.5 multiply_reduce_fusion
  777.6 11.9 %copy.74 = bf16[512,8192]{1,0:T(8,128)(2,1)} copy(bf16[512,8192]{0,1:T(8,128)(2,1)} %fusion) | data formatting | bytes 16777216
  789.5 93.8 %psum.7 = f32[]{:T(128)} all-reduce(f32[]{:T(128)} %multiply_reduce_fusion), channel_id=1, replica_groups=mesh['cuts'=8,'fsdp'=16] {'cuts','fsdp'}, use_global_device_ids=true, to_apply=%region_6.7 | all-reduce | flops 1 | bytes 8 | tf_op jit(solution)/shard_map/psum | solution.py:100
  884.1 0.8 fusion.3
  (60 shorter events, 11.4 us)
Async XLA Ops:
  7.2 52.6 %copy-start = (bf16[512,512]{1,0:T(8,128)(2,1)S(1)}, bf16[512,512]{1,0:T(8,128)(2,1)}, u32[]{:S(2)}) copy-start(bf16[512,512]{1,0:T(8,128)(2,1)} %param.9) | copy-start | bytes 1572868
  8.6 21.2 %all-to-all-start = ((f32[128,1,1]{2,1,0:T(1,128)}), f32[128,1,1]{2,1,0:T(1,128)S(1)}, u32[]{:S(2)}, u32[]{:S(2)}) async-start(f32[128,1,1]{2,1,0:T(1,128)} %copy.60), calls=%async_computation | async-start | bytes 131072 | tf_op jit(solution)/shard_map/all_to_all | solution.py:64
  29.9 21.0 %all-to-all-start.1 = ((bf16[128,2,3,256]{3,1,2,0:T(2,128)(2,1)}), bf16[128,2,3,256]{3,1,2,0:T(2,128)(2,1)S(1)}, u32[]{:S(2)}, u32[]{:S(2)}) async-start(bf16[128,2,3,256]{3,1,2,0:T(2,128)(2,1)} %copy.66), calls=%async_computation.1 | async-start | bytes 786432 | tf_op jit(solution)/shard_map/all_to_all | solution.py:61
  38.1 87.5 %all-gather.2.cloned.1.call-start = ((), (), s32[]{:S(2)}) async-start(), calls=%async_computation.4 | async-start | bytes 8454144 | tf_op jit(solution)/shard_map/all_gather | solution.py:83
  59.7 716.3 %reduce-scatter.2.cloned.1.call-start = ((), (), s32[]{:S(2)}) async-start(), calls=%async_computation.5 | async-start | bytes 16908288 | tf_op jit(solution)/shard_map/reduce_scatter | solution.py:87
  71.4 0.7 copy-start.3
  71.4 0.7 copy-start.4
  777.5 106.5 %copy-start.1 = (bf16[64,512]{1,0:T(8,128)(2,1)S(1)}, bf16[64,512]{1,0:T(8,128)(2,1)}, u32[]{:S(2)}) copy-start(bf16[64,512]{1,0:T(8,128)(2,1)} %reshape_squeeze.3) | copy-start | bytes 196612
  777.6 106.5 %copy-start.2 = (f32[64,512]{1,0:T(8,128)S(1)}, f32[64,512]{1,0:T(8,128)}, u32[]{:S(2)}) copy-start(f32[64,512]{1,0:T(8,128)} %reduce-scatter.2.cloned.1.call-done) | copy-start | bytes 393220
Sparse Core Ops, SparseCore 0:
  59.8 65.7 all-gather.1
  128.0 647.9 reduce-scatter.1
where the time goes:
time: 895 us
  waiting for transfers between devices  686 us (77%)
  blocking collectives  108 us (12%)
  local copies, waits for them, and re-layouts  34.3 us (4%)
  matrix products  21.9 us (2%)
  starting transfers between devices  19.8 us (2%)
  between operations  15.1 us (2%)
  other arithmetic  9.88 us (1%)
    reduce_scatter x1, waiting for transfers between devices, shards(): lax.psum_scatter(lax.dot_general(hidden_states, key_cotangent, (((0,), (0...  640 us
    psum x1, blocking collectives, shards(): square_sum = lax.psum(jnp.sum(gradient * gradient), ('cuts', 'fsdp'))  93.8 us
    all_gather x1, waiting for transfers between devices, shards(): lax.all_gather(own_weight, ('cuts', 'fsdp'), axis=0, tiled=True)  34 us
  transfers between devices with their start and end apart: 4, of which 4 were waited for; matrix products, arithmetic and copies ran while one was open for 4% of the time, Pallas kernels for 0%

commit v1 on v0

--- a/solution.py
+++ b/solution.py
@@ -11,6 +11,11 @@
 weight_decay = 0.1
 clip_norm = 1.0
 tiny_scale = 1e-30
+
+
+def all_by_exchange(block, mesh_axis, dim):
+    sent = jnp.stack([block] * lax.axis_size(mesh_axis))
+    return jnp.concatenate(lax.all_to_all(sent, mesh_axis, 0, 0), axis=dim)
 
 
 def adam_blocks(clipped, weight, first, first_scale, second, second_scale):
@@ -80,7 +85,7 @@
     own_weight = owned_state[:, 0].reshape(own_rows, key_width)
     input_grad = lax.dot_general(
         key_cotangent,
-        lax.all_gather(own_weight, ("cuts", "fsdp"), axis=0, tiled=True),
+        all_by_exchange(own_weight, ("cuts", "fsdp"), 0),
         (((1,), (1,)), ((), ())),
         preferred_element_type=jnp.float32,
     ).astype(jnp.bfloat16)

time: 895 us -> 834 us (0.932)
  waiting for transfers between devices: 686 us -> 626 us
  blocking collectives: 108 us -> 96.4 us
  starting transfers between devices: 19.8 us -> 29.7 us
    reduce_scatter x1, waiting for transfers between devices: 640 us -> 489 us  [shards(): lax.psum_scatter(lax.dot_general(hidden_states, key_cotangent, (((0,), (0...]
    all_to_all x0 -> x2, waiting for transfers between devices: none -> 122 us  [the longest x1 119 us: all_by_exchange(): return jnp.concatenate(lax.all_to_all(sent, mesh_axis, 0, 0), axis=dim)]
    all_gather x1 -> x0, waiting for transfers between devices: 34 us -> none  [shards(): lax.all_gather(own_weight, ('cuts', 'fsdp'), axis=0, tiled=True)]
    all_to_all x1 -> x0, blocking collectives: 14.2 us -> none  [shards(): lax.all_to_all(packed_scales, ('cuts', 'fsdp'), split_axis=0, concat_axis...]
    all_to_all x0 -> x2, starting transfers between devices: none -> 12 us  [the longest x1 7.63 us: all_by_exchange(): return jnp.concatenate(lax.all_to_all(sent, mesh_axis, 0, 0), axis=dim)]
  transfers between devices with their start and end apart: 4 -> 5, of which waited for: 4 -> 5; matrix products, arithmetic and copies ran while one was open for 4% -> 4% of each run, Pallas kernels for 0% -> 0%
where the time goes in v1:
time: 834 us; the launch traced here: 833 us
  waiting for transfers between devices  626 us (75%)
  blocking collectives  96.4 us (12%)
  local copies, waits for them, and re-layouts  36.3 us (4%)
  starting transfers between devices  29.7 us (4%)
  matrix products  21.9 us (3%)
  between operations  15.2 us (2%)
    reduce_scatter x1, waiting for transfers between devices, shards(): lax.psum_scatter(lax.dot_general(hidden_states, key_cotangent, (((0,), (0...  489 us
    all_to_all x1, waiting for transfers between devices, all_by_exchange(): return jnp.concatenate(lax.all_to_all(sent, mesh_axis, 0, 0), axis=dim)  119 us
    psum x1, blocking collectives, shards(): square_sum = lax.psum(jnp.sum(gradient * gradient), ('cuts', 'fsdp'))  96.4 us
  transfers between devices with their start and end apart: 5, of which 5 were waited for; matrix products, arithmetic and copies ran while one was open for 4% of the time, Pallas kernels for 0%

profile of v1, /device:TPU:1, one launch (start us, length us, event | category | flops | bytes accessed | tf_op | source)
XLA Modules:
  0.0 833.0 jit_solution(112604125082609523)
XLA Ops:
  7.2 1.0 copy-done
  8.2 11.7 %fusion.15 = f32[8192,512]{1,0:T(8,128)} fusion(bf16[512,8192]{1,0:T(8,128)(2,1)} %param.8, bf16[512,512]{1,0:T(8,128)(2,1)S(1)} %copy-done), kind=kOutput, calls=%fused_computation.49 | convolution fusion | flops 4294967296 | bytes 25690112 | tf_op jit(solution)/shard_map/dot_general | solution.py:93
  21.3 11.5 %all-to-all-start = ((f32[128,1,1]{2,1,0:T(1,128)}), f32[128,1,1]{2,1,0:T(1,128)S(1)}, u32[]{:S(2)}, u32[]{:S(2)}) async-start(f32[128,1,1]{2,1,0:T(1,128)} %copy.60), calls=%async_computation | async-start | bytes 131072 | tf_op jit(solution)/shard_map/all_to_all | solution.py:69
  34.3 1.2 gather_fusion
  35.5 1.1 copy.66
  37.4 1.5 copy.71
  38.9 3.6 all-to-all-done
  42.5 6.2 all-to-all-start.1
  49.0 2.4 convert_reduce_fusion
  51.6 10.9 %all-to-all-done.1 = bf16[128,2,3,256]{3,1,2,0:T(2,128)(2,1)S(1)} async-done(((bf16[128,2,3,256]{3,1,2,0:T(2,128)(2,1)}), bf16[128,2,3,256]{3,1,2,0:T(2,128)(2,1)S(1)}, u32[]{:S(2)}, u32[]{:S(2)}) %all-to-all-start.1) | async-done | bytes 393248 | tf_op jit(solution)/shard_map/all_to_all | solution.py:66
  62.5 4.4 all-to-all-start.3
  67.2 7.3 scatter_fusion
  75.1 2.6 all-to-all-done.3
  77.7 4.4 stack.28
  82.2 7.6 all-to-all-start.2
  89.8 0.9 copy.78
  90.7 1.2 scatter_custom_fusion.1
  93.2 119.4 %all-to-all-done.2 = bf16[128,64,512]{2,1,0:T(8,128)(2,1)} async-done(((bf16[128,64,512]{2,1,0:T(8,128)(2,1)}), bf16[128,64,512]{2,1,0:T(8,128)(2,1)}, u32[]{:S(2)}, u32[]{:S(2)}) %all-to-all-start.2) | async-done | bytes 8388640 | tf_op jit(solution)/shard_map/all_to_all | solution.py:18
  212.5 10.2 %fusion = bf16[512,8192]{0,1:T(8,128)(2,1)} fusion(bf16[8192,512]{1,0:T(8,128)(2,1)} %bitcast.10, bf16[512,512]{1,0:T(8,128)(2,1)S(1)} %copy-done), kind=kOutput, calls=%fused_computation.5 | convolution fusion | flops 4299161600 | bytes 17301504 | tf_op jit(solution)/shard_map/dot_general | solution.py:86
  222.8 489.1 %reduce-scatter.2.cloned.1.call-done = f32[64,512]{1,0:T(8,128)} async-done(((f32[8192,512]{1,0:T(8,128)}), f32[64,512]{1,0:T(8,128)}) %reduce-scatter.2.cloned.1.call-update) | async-done | bytes 131088 | tf_op jit(solution)/shard_map/reduce_scatter | solution.py:92
  711.9 1.5 multiply_reduce_fusion
  713.5 11.9 %copy.74 = bf16[512,8192]{1,0:T(8,128)(2,1)} copy(bf16[512,8192]{0,1:T(8,128)(2,1)} %fusion) | data formatting | bytes 16777216
  725.4 96.4 %psum.7 = f32[]{:T(128)} all-reduce(f32[]{:T(128)} %multiply_reduce_fusion), channel_id=1, replica_groups=mesh['cuts'=8,'fsdp'=16] {'cuts','fsdp'}, use_global_device_ids=true, to_apply=%region_6.7 | all-reduce | flops 1 | bytes 8 | tf_op jit(solution)/shard_map/psum | solution.py:105
  822.6 0.8 fusion.3
  (67 shorter events, 9.1 us)
Async XLA Ops:
  7.2 1.0 copy-start
  7.2 704.7 %reduce-scatter.2.cloned.1.call-start = ((), (), s32[]{:S(2)}) async-start(), calls=%async_computation.5 | async-start | bytes 16908288 | tf_op jit(solution)/shard_map/reduce_scatter | solution.py:92
  19.9 0.7 copy-start.5
  19.9 13.6 %copy-start.2 = (bf16[128,256]{1,0:T(8,128)(2,1)S(1)}, bf16[128,256]{1,0:T(8,128)(2,1)}, u32[]{:S(2)}) copy-start(bf16[128,256]{1,0:T(8,128)(2,1)} %param.10) | copy-start | bytes 196612
  19.9 13.7 %copy-start.3 = (bf16[128,256]{1,0:T(8,128)(2,1)S(1)}, bf16[128,256]{1,0:T(8,128)(2,1)}, u32[]{:S(2)}) copy-start(bf16[128,256]{1,0:T(8,128)(2,1)} %param.11) | copy-start | bytes 196612
  19.9 13.8 %copy-start.4 = (bf16[128,256]{1,0:T(8,128)(2,1)S(1)}, bf16[128,256]{1,0:T(8,128)(2,1)}, u32[]{:S(2)}) copy-start(bf16[128,256]{1,0:T(8,128)(2,1)} %param.13) | copy-start | bytes 196612
  19.9 14.4 %copy-start.6 = (f32[128]{0:T(128)S(1)}, f32[128]{0:T(128)}, u32[]{:S(2)}) copy-start(f32[128]{0:T(128)} %param.14) | copy-start | bytes 1540
  19.9 14.4 %copy-start.7 = (f32[128]{0:T(128)S(1)}, f32[128]{0:T(128)}, u32[]{:S(2)}) copy-start(f32[128]{0:T(128)} %param.12) | copy-start | bytes 1540
  21.3 21.2 %all-to-all-start = ((f32[128,1,1]{2,1,0:T(1,128)}), f32[128,1,1]{2,1,0:T(1,128)S(1)}, u32[]{:S(2)}, u32[]{:S(2)}) async-start(f32[128,1,1]{2,1,0:T(1,128)} %copy.60), calls=%async_computation | async-start | bytes 131072 | tf_op jit(solution)/shard_map/all_to_all | solution.py:69
  42.5 20.0 %all-to-all-start.1 = ((bf16[128,2,3,256]{3,1,2,0:T(2,128)(2,1)}), bf16[128,2,3,256]{3,1,2,0:T(2,128)(2,1)S(1)}, u32[]{:S(2)}, u32[]{:S(2)}) async-start(bf16[128,2,3,256]{3,1,2,0:T(2,128)(2,1)} %copy.66), calls=%async_computation.1 | async-start | bytes 786432 | tf_op jit(solution)/shard_map/all_to_all | solution.py:66
  62.5 15.2 %all-to-all-start.3 = ((f32[128,2,2]{1,2,0:T(2,128)}), f32[128,2,2]{1,2,0:T(2,128)S(1)}, u32[]{:S(2)}, u32[]{:S(2)}) async-start(f32[128,2,2]{1,2,0:T(2,128)} %copy.71), calls=%async_computation.3 | async-start | bytes 262144 | tf_op jit(solution)/shard_map/all_to_all | solution.py:68
  82.2 130.4 %all-to-all-start.2 = ((bf16[128,64,512]{2,1,0:T(8,128)(2,1)}), bf16[128,64,512]{2,1,0:T(8,128)(2,1)}, u32[]{:S(2)}, u32[]{:S(2)}) async-start(bf16[128,64,512]{2,1,0:T(8,128)(2,1)} %stack.28), calls=%async_computation.2 | async-start | bytes 16777216 | tf_op jit(solution)/shard_map/all_to_all | solution.py:18
  713.5 109.1 %copy-start.1 = (f32[64,512]{1,0:T(8,128)S(1)}, f32[64,512]{1,0:T(8,128)}, u32[]{:S(2)}) copy-start(f32[64,512]{1,0:T(8,128)} %reduce-scatter.2.cloned.1.call-done) | copy-start | bytes 393220
Sparse Core Ops, SparseCore 0:
  20.1 691.8 reduce-scatter.1
